TPU v7x, 512 devices: a whole 4x8x8 slice. The times are simulated.
512 devices in a mesh: row: 8 (over z), col: 16 (over y, core), vox: 4 (over x).
Axes of the slice: x: 4, y: 8, z: 8, core: 2. Of those that a mesh axis runs over, the one named last changes fastest.
Arguments:
- panel_top: bfloat16 [1024, 1024], P('row', ('col', 'vox')), may hold values from -0.059814453 to 0.059814453
- panel_low: bfloat16 [8192, 1024], P('row', ('col', 'vox')), may hold values from -1.1953125 to 1.1953125
- panel_next: bfloat16 [8192, 1024], P('row', ('col', 'vox')), may hold values from -1.1953125 to 1.1953125
- gram_rest: bfloat16 [8192, 8192], P('row', ('col', 'vox')), may hold values from -18 to 18
- inverses: bfloat16 [2, 1024, 1024], P(None, 'row'), as said below
- right_top: bfloat16 [2, 1024, 8192], P(None, None, ('col', 'vox')), may hold values from -1.796875 to 1.796875
- right_low: bfloat16 [8192, 8192], P('row', ('col', 'vox')), may hold values from -24 to 24
Outputs:
- factor: bfloat16 [2, 8192, 1024], P(None, 'row', ('col', 'vox'))
- solved: bfloat16 [2, 1024, 8192], P(None, None, ('col', 'vox'))
- trailing: float32 [8192, 8192], P('row', ('col', 'vox'))
- residual: float32 [8192, 8192], P('row', ('col', 'vox'))
Inputs may be any that keep to these rules, and one draw needn't show every extreme that they name: Each inverses[k] is lower triangular with diagonal entries from 1 to 2.
All inputs are finite; a program needn't handle non-finite values.
Results may differ from a plain program's by a relative error of at most 0.0057.
Values may be sent and summed in bfloat16 or wider, within the bound.
No kernel may reach another device: no remote copies, remote signals or barrier semaphores. Data moves between devices by JAX's collectives and lax.ppermute only.
A program may use at most 64 MiB of HBM per device.

v0:
```python
import jax
import jax.numpy as jnp
import numpy as np
from jax import lax
from jax.sharding import Mesh
from jax.sharding import PartitionSpec as P


def contract(left, right, dims):
    return lax.dot_general(left, right, (dims, ((), ())), preferred_element_type=jnp.float32)


def gather_small(block, axis, size):
    out = lax.all_to_all(jnp.tile(block, (size, 1)), axis, 0, 0, tiled=True)
    return out.reshape((size,) + block.shape)


def per_device(sizes, panel_top, panel_low, panel_next, gram_rest, inverses, right_top, right_low):
    rows, ys, cores, voxes = sizes
    axes = ("row", "y", "core", "vox")
    order = np.arange(rows * ys * cores * voxes).reshape(sizes)
    swap = list(zip(order.ravel().tolist(), order.transpose(1, 0, 2, 3).ravel().tolist()))
    y = lax.axis_index("y")
    core = lax.axis_index("core")
    vox = lax.axis_index("vox")
    width = panel_low.shape[1]
    rest_cols = gram_rest.shape[1]
    bf16 = jnp.bfloat16
    whole = lax.all_gather(inverses, "row", axis=1, tiled=True)
    top = gather_small(panel_top.T, "row", rows).transpose(1, 0, 2).reshape(width, -1)
    panels = jnp.stack([top, panel_low.T, panel_next.T])
    panels = lax.all_gather(panels, ("y", "core", "vox"), axis=1, tiled=True)
    low = panels[0:2].transpose(1, 0, 2).reshape(panels.shape[1], -1)
    first = contract(whole[0], low, ((1,), (0,))).astype(bf16)
    first_top, first_low = (first[:, : panels.shape[2]], first[:, panels.shape[2] :])
    updated = (panels[2].astype(jnp.float32) - contract(first_top, first_low, ((0,), (0,)))).astype(
        bf16
    )
    second_low = contract(whole[1], updated, ((1,), (0,))).astype(bf16)
    start = (core * voxes + vox) * rest_cols
    first_rows = lax.ppermute(lax.dynamic_slice_in_dim(first_low, start, rest_cols, 1), axes, swap)
    second_rows = lax.ppermute(
        lax.dynamic_slice_in_dim(second_low, start, rest_cols, 1), axes, swap
    )
    first_solve = contract(whole[0], right_top[0], ((1,), (0,))).astype(bf16)
    top_new = (
        right_top[1].astype(jnp.float32) - contract(first_top, first_solve, ((0,), (0,)))
    ).astype(bf16)
    second_solve = contract(whole[1], top_new, ((1,), (0,))).astype(bf16)
    residual = (
        right_low.astype(jnp.float32)
        - contract(first_low, first_solve, ((0,), (0,)))
        - contract(second_low, second_solve, ((0,), (0,)))
    )
    trailing = (
        gram_rest.astype(jnp.float32)
        - contract(first_low, first_rows, ((0,), (0,)))
        - contract(second_low, second_rows, ((0,), (0,)))
    )
    own = ((y * cores + core) * voxes + vox) * width
    factor = jnp.stack(
        [
            lax.dynamic_slice_in_dim(first_low, own, width, 0).T,
            lax.dynamic_slice_in_dim(second_low, own, width, 0).T,
        ]
    )
    solved = jnp.stack([first_solve, second_solve])
    return (factor, solved, trailing, residual)


def solution(mesh):
    cores = 2
    sizes = (mesh.shape["row"], mesh.shape["col"] // cores, cores, mesh.shape["vox"])
    split = Mesh(mesh.devices.reshape(sizes), ("row", "y", "core", "vox"))
    cols = ("y", "core", "vox")
    in_specs = (
        P("row", cols),
        P("row", cols),
        P("row", cols),
        P("row", cols),
        P(None, "row", None),
        P(None, None, cols),
        P("row", cols),
    )
    out_specs = (P(None, "row", cols), P(None, None, cols), P("row", cols), P("row", cols))

    def body(*args):
        return per_device(sizes, *args)

    return jax.shard_map(body, mesh=split, in_specs=in_specs, out_specs=out_specs, check_vma=False)
```

profile of v0, /device:TPU:16, one launch (start us, length us, event | category | flops | bytes accessed | tf_op | source)
XLA Modules:
  0.0 259.9 jit_solution(18153763955404550325)
XLA Ops:
  8.6 18.1 %all_to_all.6 = bf16[8,16,128]{2,1,0:T(8,128)(2,1)S(1)} all-to-all(bf16[8,16,128]{2,1,0:T(8,128)(2,1)S(1)} %tile.2), channel_id=1, replica_groups=mesh['row'=8,'y'=8,'core'=2,'vox'=4] {'row'}, dimensions={0} | all-to-all | bytes 65536 | tf_op jit(solution)/shard_map/all_to_all | solution.py:14
  26.8 1.4 pad_maximum_fusion.1
  28.3 44.6 %all-gather.5.cloned.1.call-done = bf16[2,1024,1024]{2,1,0:T(8,128)(2,1)} async-done(((bf16[2,128,1024]{2,1,0:T(8,128)(2,1)}), bf16[2,1024,1024]{2,1,0:T(8,128)(2,1)}) %all-gather.5.cloned.1.call-update) | async-done | bytes 4194320 | tf_op jit(solution)/shard_map/all_gather | solution.py:29
  72.9 2.3 fusion.17
  75.2 85.2 %all-gather.3.cloned.1.call-done = bf16[3,1024,1024]{2,1,0:T(8,128)(2,1)} async-done(((bf16[3,16,1024]{2,1,0:T(8,128)(2,1)}), bf16[3,1024,1024]{2,1,0:T(8,128)(2,1)}) %all-gather.3.cloned.1.call-update) | async-done | bytes 6291472 | tf_op jit(solution)/shard_map/all_gather | solution.py:32
  160.4 4.7 %slice.34 = bf16[2,1024,1024]{2,1,0:T(8,128)(2,1)} slice(bf16[3,1024,1024]{2,1,0:T(8,128)(2,1)} %all-gather.3.cloned.1.call-done), slice={[0:2], [0:1024], [0:1024]} | slice | bytes 8388608 | tf_op jit(solution)/shard_map/slice | solution.py:33
  165.1 6.2 %copy.22 = bf16[2,1024,1024]{1,2,0:T(8,128)(2,1)} copy(bf16[2,1024,1024]{2,1,0:T(8,128)(2,1)} %slice.34) | data formatting | bytes 8388608
  171.3 7.4 %convert_bitcast_fusion = bf16[1024,2048]{1,0:T(8,128)(2,1)S(1)} fusion(bf16[1024,2048]{0,1:T(8,128)(2,1)} %bitcast.62, bf16[2,1024,1024]{2,1,0:T(8,128)(2,1)} %all-gather.5.cloned.1.call-done), kind=kOutput, calls=%fused_computation.2 | convolution fusion | flops 4297064448 | bytes 10485760 | tf_op jit(solution)/shard_map/dot_general | solution.py:10
  178.7 2.0 copy-done
  180.7 1.5 slice.36
  182.2 8.0 %fusion.3 = bf16[1024,1024]{0,1:T(8,128)(2,1)S(1)} fusion(bf16[3,1024,1024]{2,1,0:T(8,128)(2,1)} %all-gather.3.cloned.1.call-done, bf16[2,1024,1024]{2,1,0:T(8,128)(2,1)} %all-gather.5.cloned.1.call-done, bf16[1024,2048]{1,0:T(8,128)(2,1)} %copy-done), kind=kOutput, calls=%fused_computation.7 | convolution fusion | flops 4299161600 | bytes 10485760 | tf_op jit(solution)/shard_map/dot_general | solution.py:10
  190.2 0.8 dynamic-slice_bitcast_fusion.2
  191.0 0.8 dynamic-slice_bitcast_fusion
  191.8 1.0 constant_dynamic-slice_fusion
  192.8 5.5 %collective-permute-start.1 = (bf16[1024,128]{1,0:T(8,128)(2,1)}, bf16[1024,128]{1,0:T(8,128)(2,1)S(1)}, u32[]{:S(2)}, u32[]{:S(2)}) collective-permute-start(bf16[1024,128]{1,0:T(8,128)(2,1)} %dynamic-slice_bitcast_fusion), channel_id=1, source_target_pairs={{0,0},{1,1},{2,2},{3,3},{4,4},{5,5},{6,6},{7,7},{8,64},{9,65},{10,... | collective-permute-start | bytes 786440 | tf_op jit(solution)/shard_map/ppermute | solution.py:42
  198.2 3.2 %collective-permute-start = (bf16[1024,128]{1,0:T(8,128)(2,1)S(1)}, bf16[1024,128]{1,0:T(8,128)(2,1)}, u32[]{:S(2)}, u32[]{:S(2)}) collective-permute-start(bf16[1024,128]{1,0:T(8,128)(2,1)S(1)} %constant_dynamic-slice_fusion), channel_id=1, source_target_pairs={{0,0},{1,1},{2,2},{3,3},{4,4},{5,5},{6,6},{7,7},{8,64},{9,65},{10,... | collective-permute-start | bytes 786440 | tf_op jit(solution)/shard_map/ppermute | solution.py:41
  202.1 2.3 convolution_subtract_fusion.1
  204.5 4.5 %fusion.16 = bf16[128,1024]{0,1:T(8,128)(2,1)S(1)} fusion(bf16[2,1024,1024]{2,1,0:T(8,128)(2,1)} %all-gather.5.cloned.1.call-done, bf16[1024,128]{1,0:T(8,128)(2,1)} %copy-done.2, bf16[1024,2048]{1,0:T(8,128)(2,1)} %copy-done, bf16[2,1024,128]{2,1,0:T(8,128)(2,1)} %param.12), kind=kOutput, calls=%fused_computation.19 | convolution fusion | flops 537395200 | bytes 4980736 | tf_op jit(solution)/shard_map/dot_general | solution.py:10
  209.0 1.8 pad_maximum_fusion
  210.8 1.5 convolution_subtract_fusion
  212.3 33.1 %collective-permute-done.1 = bf16[1024,128]{1,0:T(8,128)(2,1)S(1)} collective-permute-done((bf16[1024,128]{1,0:T(8,128)(2,1)}, bf16[1024,128]{1,0:T(8,128)(2,1)S(1)}, u32[]{:S(2)}, u32[]{:S(2)}) %collective-permute-start.1) | collective-permute-done | bytes 262176 | tf_op jit(solution)/shard_map/ppermute | solution.py:42
  245.4 0.7 fusion.36
  246.2 4.4 %collective-permute-done = bf16[1024,128]{1,0:T(8,128)(2,1)} collective-permute-done((bf16[1024,128]{1,0:T(8,128)(2,1)S(1)}, bf16[1024,128]{1,0:T(8,128)(2,1)}, u32[]{:S(2)}, u32[]{:S(2)}) %collective-permute-start) | collective-permute-done | bytes 262176 | tf_op jit(solution)/shard_map/ppermute | solution.py:41
  250.6 2.5 fusion.15
  (16 shorter events, 2.2 us)
Async XLA Ops:
  7.2 65.7 %all-gather.5.cloned.1.call-start = ((), (), s32[]{:S(2)}) async-start(), calls=%async_computation.2 | async-start | bytes 4718592 | tf_op jit(solution)/shard_map/all_gather | solution.py:29
  7.9 152.5 %all-gather.3.cloned.1.call-start = ((), (), s32[]{:S(2)}) async-start(), calls=%async_computation.1 | async-start | bytes 6389760 | tf_op jit(solution)/shard_map/all_gather | solution.py:32
  75.2 127.0 %copy-start.2 = (bf16[1024,128]{1,0:T(8,128)(2,1)}, bf16[1024,128]{1,0:T(8,128)(2,1)S(1)}, u32[]{:S(2)}) copy-start(bf16[1024,128]{1,0:T(8,128)(2,1)S(1)} %fusion.17) | copy-start | bytes 786436
  178.7 2.1 copy-start
  192.8 52.7 %collective-permute-start.1 = (bf16[1024,128]{1,0:T(8,128)(2,1)}, bf16[1024,128]{1,0:T(8,128)(2,1)S(1)}, u32[]{:S(2)}, u32[]{:S(2)}) collective-permute-start(bf16[1024,128]{1,0:T(8,128)(2,1)} %dynamic-slice_bitcast_fusion), channel_id=1, source_target_pairs={{0,0},{1,1},{2,2},{3,3},{4,4},{5,5},{6,6},{7,7},{8,64},{9,65},{10,... | collective-permute-start | bytes 786440 | tf_op jit(solution)/shard_map/ppermute | solution.py:42
  198.2 52.3 %collective-permute-start = (bf16[1024,128]{1,0:T(8,128)(2,1)S(1)}, bf16[1024,128]{1,0:T(8,128)(2,1)}, u32[]{:S(2)}, u32[]{:S(2)}) collective-permute-start(bf16[1024,128]{1,0:T(8,128)(2,1)S(1)} %constant_dynamic-slice_fusion), channel_id=1, source_target_pairs={{0,0},{1,1},{2,2},{3,3},{4,4},{5,5},{6,6},{7,7},{8,64},{9,65},{10,... | collective-permute-start | bytes 786440 | tf_op jit(solution)/shard_map/ppermute | solution.py:41
  210.8 39.7 %copy-start.1 = (bf16[1024,2048]{1,0:T(8,128)(2,1)S(1)}, bf16[1024,2048]{1,0:T(8,128)(2,1)}, u32[]{:S(2)}) copy-start(bf16[1024,2048]{1,0:T(8,128)(2,1)} %copy-done) | copy-start | bytes 12582916
  210.8 39.7 %copy-start.3 = (bf16[1024,128]{1,0:T(8,128)(2,1)S(1)}, bf16[1024,128]{1,0:T(8,128)(2,1)}, u32[]{:S(2)}) copy-start(bf16[1024,128]{1,0:T(8,128)(2,1)} %param.10) | copy-start | bytes 786436
Sparse Core Ops, SparseCore 0:
  10.1 62.7 all-gather.4
  76.8 83.5 all-gather.2
where the time goes:
time: 261 us; the launch traced here: 260 us
  waiting for transfers between devices  168 us (64%)
  matrix products  29.4 us (11%)
  blocking collectives  18.1 us (7%)
  local copies, waits for them, and re-layouts  17.6 us (7%)
  between operations  14.1 us (5%)
  starting transfers between devices  8.8 us (3%)
  other arithmetic  3.86 us (1%)
    all_gather x1, waiting for transfers between devices, per_device(): panels = lax.all_gather(panels, ('y', 'core', 'vox'), axis=1, tiled=True)  85.2 us
    all_gather x1, waiting for transfers between devices, per_device(): whole = lax.all_gather(inverses, 'row', axis=1, tiled=True)  44.6 us
    ppermute x1, waiting for transfers between devices, per_device(): lax.ppermute(lax.dynamic_slice_in_dim(second_low, start, rest_cols, 1), a...  33.1 us
    dot_general x8, matrix products, contract(): lax.dot_general(left, right, (dims, ((), ())), preferred_element_type=jnp...  29.4 us
    all_to_all x1, blocking collectives, gather_small(): out = lax.all_to_all(jnp.tile(block, (size, 1)), axis, 0, 0, tiled=True)  18.1 us
    unnamed x9, local copies, waits for them, and re-layouts  8.24 us
    ppermute x1, starting transfers between devices, per_device(): lax.ppermute(lax.dynamic_slice_in_dim(second_low, start, rest_cols, 1), a...  5.48 us
  transfers between devices with their start and end apart: 4, of which 4 were waited for; matrix products, arithmetic and copies ran while one was open for 6% of the time, Pallas kernels for 0%

commit v1 on v0

--- a/solution.py
+++ b/solution.py
@@ -26,7 +26,16 @@
     width = panel_low.shape[1]
     rest_cols = gram_rest.shape[1]
     bf16 = jnp.bfloat16
-    whole = lax.all_gather(inverses, "row", axis=1, tiled=True)
+    ways = lax.axis_size("row")
+    up = [(d, (d + 1) % ways) for d in range(ways)]
+    down = [(d, (d - 1) % ways) for d in range(ways)]
+    earlier, later = ([inverses], [inverses])
+    for _ in range(ways // 2):
+        earlier.append(lax.ppermute(earlier[-1], "row", up))
+    for _ in range((ways - 1) // 2):
+        later.append(lax.ppermute(later[-1], "row", down))
+    line = jnp.concatenate([*earlier[::-1], *later[1:]], axis=1)
+    whole = jnp.roll(line, (lax.axis_index("row") - ways // 2) * inverses.shape[1], axis=1)
     top = gather_small(panel_top.T, "row", rows).transpose(1, 0, 2).reshape(width, -1)
     panels = jnp.stack([top, panel_low.T, panel_next.T])
     panels = lax.all_gather(panels, ("y", "core", "vox"), axis=1, tiled=True)

time: 261 us -> 210 us (0.80)
  waiting for transfers between devices: 168 us -> 95.4 us
  starting transfers between devices: 8.8 us -> 32.6 us
  matrix products: 29.4 us -> 25.2 us
  local copies, waits for them, and re-layouts: 17.6 us -> 20.9 us
    all_gather x1, waiting for transfers between devices: 85.2 us -> 19.8 us  [per_device(): panels = lax.all_gather(panels, ('y', 'core', 'vox'), axis=1, tiled=True)]
    all_gather x1 -> x0, waiting for transfers between devices: 44.6 us -> none  [per_device(): whole = lax.all_gather(inverses, 'row', axis=1, tiled=True)]
    ppermute x0 -> x7, waiting for transfers between devices: none -> 32.1 us  [the longest x4 32.1 us: per_device(): earlier.append(lax.ppermute(earlier[-1], 'row', up))]
    ppermute x0 -> x7, starting transfers between devices: none -> 23.7 us  [the longest x3 15.5 us: per_device(): later.append(lax.ppermute(later[-1], 'row', down))]
    ppermute x1, waiting for transfers between devices: 33.1 us -> 38.6 us  [per_device(): lax.ppermute(lax.dynamic_slice_in_dim(second_low, start, rest_cols, 1), a...]
    dot_general x8, matrix products: 29.4 us -> 25.2 us  [contract(): lax.dot_general(left, right, (dims, ((), ())), preferred_element_type=jnp...]
    unnamed x9 -> x32, local copies, waits for them, and re-layouts: 8.24 us -> 12.1 us
  transfers between devices with their start and end apart: 4 -> 10, of which waited for: 4 -> 7; matrix products, arithmetic and copies ran while one was open for 6% -> 4% of each run, Pallas kernels for 0% -> 0%
where the time goes in v1:
time: 210 us
  waiting for transfers between devices  95.4 us (45%)
  starting transfers between devices  32.6 us (16%)
  matrix products  25.2 us (12%)
  local copies, waits for them, and re-layouts  20.9 us (10%)
  blocking collectives  18.1 us (9%)
  between operations  14.4 us (7%)
  other arithmetic  2.91 us (1%)
    ppermute x1, waiting for transfers between devices, per_device(): lax.ppermute(lax.dynamic_slice_in_dim(second_low, start, rest_cols, 1), a...  38.6 us
    ppermute x4, waiting for transfers between devices, per_device(): earlier.append(lax.ppermute(earlier[-1], 'row', up))  32.1 us
    dot_general x8, matrix products, contract(): lax.dot_general(left, right, (dims, ((), ())), preferred_element_type=jnp...  25.2 us
    all_gather x1, waiting for transfers between devices, per_device(): panels = lax.all_gather(panels, ('y', 'core', 'vox'), axis=1, tiled=True)  19.8 us
    all_to_all x1, blocking collectives, gather_small(): out = lax.all_to_all(jnp.tile(block, (size, 1)), axis, 0, 0, tiled=True)  18.1 us
    ppermute x3, starting transfers between devices, per_device(): later.append(lax.ppermute(later[-1], 'row', down))  15.5 us
    unnamed x32, local copies, waits for them, and re-layouts  12.1 us
    ppermute x4, starting transfers between devices, per_device(): earlier.append(lax.ppermute(earlier[-1], 'row', up))  8.2 us
  transfers between devices with their start and end apart: 10, of which 7 were waited for; matrix products, arithmetic and copies ran while one was open for 4% of the time, Pallas kernels for 0%

profile of v1, /device:TPU:16, one launch (start us, length us, event | category | flops | bytes accessed | tf_op | source)
XLA Modules:
  0.0 209.5 jit_solution(17943260075409718263)
XLA Ops:
  7.9 18.1 %all_to_all.6 = bf16[8,16,128]{2,1,0:T(8,128)(2,1)S(1)} all-to-all(bf16[8,16,128]{2,1,0:T(8,128)(2,1)S(1)} %tile.2), channel_id=1, replica_groups=mesh['row'=8,'y'=8,'core'=2,'vox'=4] {'row'}, dimensions={0} | all-to-all | bytes 65536 | tf_op jit(solution)/shard_map/all_to_all | solution.py:14
  27.5 2.5 %collective-permute-start = (bf16[2,128,1024]{2,1,0:T(8,128)(2,1)}, bf16[2,128,1024]{2,1,0:T(8,128)(2,1)S(1)}, u32[]{:S(2)}, u32[]{:S(2)}) collective-permute-start(bf16[2,128,1024]{2,1,0:T(8,128)(2,1)} %param.11), channel_id=1, source_target_pairs={{0,64},{64,128},{128,192},{192,256},{256,320},{320,384},{384,448},... | collective-permute-start | bytes 1572872 | tf_op jit(solution)/shard_map/ppermute | solution.py:34
  30.0 13.1 %collective-permute-done = bf16[2,128,1024]{2,1,0:T(8,128)(2,1)S(1)} collective-permute-done((bf16[2,128,1024]{2,1,0:T(8,128)(2,1)}, bf16[2,128,1024]{2,1,0:T(8,128)(2,1)S(1)}, u32[]{:S(2)}, u32[]{:S(2)}) %collective-permute-start) | collective-permute-done | bytes 524320 | tf_op jit(solution)/shard_map/ppermute | solution.py:34
  43.1 1.9 collective-permute-start.1
  45.0 5.1 %collective-permute-start.4 = (bf16[2,128,1024]{2,1,0:T(8,128)(2,1)}, bf16[2,128,1024]{2,1,0:T(8,128)(2,1)S(1)}, u32[]{:S(2)}, u32[]{:S(2)}) collective-permute-start(bf16[2,128,1024]{2,1,0:T(8,128)(2,1)} %param.11), channel_id=1, source_target_pairs={{0,448},{64,0},{128,64},{192,128},{256,192},{320,256},{384,320},{4... | collective-permute-start | bytes 1572872 | tf_op jit(solution)/shard_map/ppermute | solution.py:36
  50.1 7.3 %collective-permute-done.1 = bf16[2,128,1024]{2,1,0:T(8,128)(2,1)S(1)} collective-permute-done((bf16[2,128,1024]{2,1,0:T(8,128)(2,1)S(1)}, bf16[2,128,1024]{2,1,0:T(8,128)(2,1)S(1)}, u32[]{:S(2)}, u32[]{:S(2)}) %collective-permute-start.1) | collective-permute-done | bytes 524320 | tf_op jit(solution)/shard_map/ppermute | solution.py:34
  57.5 1.9 collective-permute-start.2
  59.4 5.1 %collective-permute-start.5 = (bf16[2,128,1024]{2,1,0:T(8,128)(2,1)S(1)}, bf16[2,128,1024]{2,1,0:T(8,128)(2,1)S(1)}, u32[]{:S(2)}, u32[]{:S(2)}) collective-permute-start(bf16[2,128,1024]{2,1,0:T(8,128)(2,1)S(1)} %collective-permute-done.4), channel_id=1, source_target_pairs={{0,448},{64,0},{128,64},{192,128},{256,192},{320,256},{384,320},{4... | collective-permute-start | bytes 1572872 | tf_op jit(solution)/shard_map/ppermute | solution.py:36
  64.5 6.4 %collective-permute-done.2 = bf16[2,128,1024]{2,1,0:T(8,128)(2,1)S(1)} collective-permute-done((bf16[2,128,1024]{2,1,0:T(8,128)(2,1)S(1)}, bf16[2,128,1024]{2,1,0:T(8,128)(2,1)S(1)}, u32[]{:S(2)}, u32[]{:S(2)}) %collective-permute-start.2) | collective-permute-done | bytes 524320 | tf_op jit(solution)/shard_map/ppermute | solution.py:34
  71.0 1.9 collective-permute-start.3
  72.9 5.3 %collective-permute-start.6 = (bf16[2,128,1024]{2,1,0:T(8,128)(2,1)S(1)}, bf16[2,128,1024]{2,1,0:T(8,128)(2,1)S(1)}, u32[]{:S(2)}, u32[]{:S(2)}) collective-permute-start(bf16[2,128,1024]{2,1,0:T(8,128)(2,1)S(1)} %collective-permute-done.5), channel_id=1, source_target_pairs={{0,448},{64,0},{128,64},{192,128},{256,192},{320,256},{384,320},{4... | collective-permute-start | bytes 1572872 | tf_op jit(solution)/shard_map/ppermute | solution.py:36
  78.2 5.3 %collective-permute-done.3 = bf16[2,128,1024]{2,1,0:T(8,128)(2,1)S(1)} collective-permute-done((bf16[2,128,1024]{2,1,0:T(8,128)(2,1)S(1)}, bf16[2,128,1024]{2,1,0:T(8,128)(2,1)S(1)}, u32[]{:S(2)}, u32[]{:S(2)}) %collective-permute-start.3) | collective-permute-done | bytes 524320 | tf_op jit(solution)/shard_map/ppermute | solution.py:34
  85.4 3.2 %copy-done.3 = bf16[2,2048,1024]{2,1,0:T(8,128)(2,1)} copy-done((bf16[2,2048,1024]{2,1,0:T(8,128)(2,1)}, bf16[2,2048,1024]{2,1,0:T(8,128)(2,1)S(1)}, u32[]{:S(2)}) %copy-start.3) | copy-done | bytes 8388632
  89.3 19.8 %all-gather.2.cloned.1.call-done = bf16[3,1024,1024]{2,1,0:T(8,128)(2,1)} async-done(((bf16[3,16,1024]{2,1,0:T(8,128)(2,1)}), bf16[3,1024,1024]{2,1,0:T(8,128)(2,1)}) %all-gather.2.cloned.1.call-update) | async-done | bytes 6291472 | tf_op jit(solution)/shard_map/all_gather | solution.py:41
  109.1 4.6 %slice.34 = bf16[2,1024,1024]{2,1,0:T(8,128)(2,1)} slice(bf16[3,1024,1024]{2,1,0:T(8,128)(2,1)} %all-gather.2.cloned.1.call-done), slice={[0:2], [0:1024], [0:1024]} | slice | bytes 8388608 | tf_op jit(solution)/shard_map/slice | solution.py:42
  113.7 6.2 %copy.17 = bf16[2,1024,1024]{1,2,0:T(8,128)(2,1)} copy(bf16[2,1024,1024]{2,1,0:T(8,128)(2,1)} %slice.34) | data formatting | bytes 8388608
  120.0 7.4 %convolution_convert_fusion = bf16[1024,2048]{1,0:T(8,128)(2,1)S(1)} fusion(bf16[1024,2048]{0,1:T(8,128)(2,1)} %bitcast.58, bf16[2,2048,1024]{2,1,0:T(8,128)(2,1)} %copy-done.3, s32[]{:T(128)S(6)} %select_n.22), kind=kOutput, calls=%fused_computation.2 | convolution fusion | flops 4297064448 | bytes 10485764 | tf_op jit(solution)/shard_map/dot_general | solution.py:10
  127.4 1.6 slice.35
  130.7 4.5 %fusion.16 = bf16[1024,128]{1,0:T(8,128)(2,1)S(1)} fusion(bf16[2,2048,1024]{2,1,0:T(8,128)(2,1)} %copy-done.3, s32[]{:T(128)S(6)} %add.35, s32[]{:T(128)S(6)} %select_n.22, bf16[1024,128]{1,0:T(8,128)(2,1)S(1)} %fusion.17, bf16[1024,2048]{1,0:T(8,128)(2,1)} %copy-done.1, bf16[2,1024,128]{2,1,0:T(8,128)(2,1)S(1)} %copy-done.5), kind=kOutput, calls=%fused_computation.19 | convolution fusion | flops 537395200 | bytes 4980744 | tf_op jit(solution)/shard_map/dot_general | solution.py:10
  135.2 8.0 %fusion.3 = bf16[1024,1024]{1,0:T(8,128)(2,1)S(1)} fusion(bf16[3,1024,1024]{2,1,0:T(8,128)(2,1)} %all-gather.2.cloned.1.call-done, bf16[2,2048,1024]{2,1,0:T(8,128)(2,1)} %copy-done.3, s32[]{:T(128)S(6)} %add.35, s32[]{:T(128)S(6)} %select_n.22, bf16[1024,2048]{1,0:T(8,128)(2,1)} %copy-done.1), kind=kOutput, calls=%fused_computation.7 | convolution fusion | flops 4299161600 | bytes 10485768 | tf_op jit(solution)/shard_map/dot_general | solution.py:10
  143.4 5.7 %collective-permute-start.8 = (bf16[1024,128]{1,0:T(8,128)(2,1)S(1)}, bf16[1024,128]{1,0:T(8,128)(2,1)S(1)}, u32[]{:S(2)}, u32[]{:S(2)}) collective-permute-start(bf16[1024,128]{1,0:T(8,128)(2,1)S(1)} %constant_dynamic-slice_fusion), channel_id=1, source_target_pairs={{0,0},{1,1},{2,2},{3,3},{4,4},{5,5},{6,6},{7,7},{8,64},{9,65},{10,... | collective-permute-start | bytes 786440 | tf_op jit(solution)/shard_map/ppermute | solution.py:51
  150.1 3.1 %collective-permute-start.7 = (bf16[1024,128]{1,0:T(8,128)(2,1)S(1)}, bf16[1024,128]{1,0:T(8,128)(2,1)S(1)}, u32[]{:S(2)}, u32[]{:S(2)}) collective-permute-start(bf16[1024,128]{1,0:T(8,128)(2,1)S(1)} %constant_dynamic-slice_fusion.1), channel_id=1, source_target_pairs={{0,0},{1,1},{2,2},{3,3},{4,4},{5,5},{6,6},{7,7},{8,64},{9,65},{10,... | collective-permute-start | bytes 786440 | tf_op jit(solution)/shard_map/ppermute | solution.py:50
  156.9 38.6 %collective-permute-done.8 = bf16[1024,128]{1,0:T(8,128)(2,1)S(1)} collective-permute-done((bf16[1024,128]{1,0:T(8,128)(2,1)S(1)}, bf16[1024,128]{1,0:T(8,128)(2,1)S(1)}, u32[]{:S(2)}, u32[]{:S(2)}) %collective-permute-start.8) | collective-permute-done | bytes 262176 | tf_op jit(solution)/shard_map/ppermute | solution.py:51
  196.3 4.9 %collective-permute-done.7 = bf16[1024,128]{1,0:T(8,128)(2,1)S(1)} collective-permute-done((bf16[1024,128]{1,0:T(8,128)(2,1)S(1)}, bf16[1024,128]{1,0:T(8,128)(2,1)S(1)}, u32[]{:S(2)}, u32[]{:S(2)}) %collective-permute-start.7) | collective-permute-done | bytes 262176 | tf_op jit(solution)/shard_map/ppermute | solution.py:50
  (50 shorter events, 13.5 us)
Async XLA Ops:
  7.2 102.0 %all-gather.2.cloned.1.call-start = ((), (), s32[]{:S(2)}) async-start(), calls=%async_computation.1 | async-start | bytes 6389760 | tf_op jit(solution)/shard_map/all_gather | solution.py:41
  27.5 15.6 %collective-permute-start = (bf16[2,128,1024]{2,1,0:T(8,128)(2,1)}, bf16[2,128,1024]{2,1,0:T(8,128)(2,1)S(1)}, u32[]{:S(2)}, u32[]{:S(2)}) collective-permute-start(bf16[2,128,1024]{2,1,0:T(8,128)(2,1)} %param.11), channel_id=1, source_target_pairs={{0,64},{64,128},{128,192},{192,256},{256,320},{320,384},{384,448},... | collective-permute-start | bytes 1572872 | tf_op jit(solution)/shard_map/ppermute | solution.py:34
  43.1 14.4 %collective-permute-start.1 = (bf16[2,128,1024]{2,1,0:T(8,128)(2,1)S(1)}, bf16[2,128,1024]{2,1,0:T(8,128)(2,1)S(1)}, u32[]{:S(2)}, u32[]{:S(2)}) collective-permute-start(bf16[2,128,1024]{2,1,0:T(8,128)(2,1)S(1)} %collective-permute-done), channel_id=1, source_target_pairs={{0,64},{64,128},{128,192},{192,256},{256,320},{320,384},{384,448},... | collective-permute-start | bytes 1572872 | tf_op jit(solution)/shard_map/ppermute | solution.py:34
  45.0 14.4 %collective-permute-start.4 = (bf16[2,128,1024]{2,1,0:T(8,128)(2,1)}, bf16[2,128,1024]{2,1,0:T(8,128)(2,1)S(1)}, u32[]{:S(2)}, u32[]{:S(2)}) collective-permute-start(bf16[2,128,1024]{2,1,0:T(8,128)(2,1)} %param.11), channel_id=1, source_target_pairs={{0,448},{64,0},{128,64},{192,128},{256,192},{320,256},{384,320},{4... | collective-permute-start | bytes 1572872 | tf_op jit(solution)/shard_map/ppermute | solution.py:36
  57.5 13.5 %collective-permute-start.2 = (bf16[2,128,1024]{2,1,0:T(8,128)(2,1)S(1)}, bf16[2,128,1024]{2,1,0:T(8,128)(2,1)S(1)}, u32[]{:S(2)}, u32[]{:S(2)}) collective-permute-start(bf16[2,128,1024]{2,1,0:T(8,128)(2,1)S(1)} %collective-permute-done.1), channel_id=1, source_target_pairs={{0,64},{64,128},{128,192},{192,256},{256,320},{320,384},{384,448},... | collective-permute-start | bytes 1572872 | tf_op jit(solution)/shard_map/ppermute | solution.py:34
  59.4 13.5 %collective-permute-start.5 = (bf16[2,128,1024]{2,1,0:T(8,128)(2,1)S(1)}, bf16[2,128,1024]{2,1,0:T(8,128)(2,1)S(1)}, u32[]{:S(2)}, u32[]{:S(2)}) collective-permute-start(bf16[2,128,1024]{2,1,0:T(8,128)(2,1)S(1)} %collective-permute-done.4), channel_id=1, source_target_pairs={{0,448},{64,0},{128,64},{192,128},{256,192},{320,256},{384,320},{4... | collective-permute-start | bytes 1572872 | tf_op jit(solution)/shard_map/ppermute | solution.py:36
  71.0 12.6 %collective-permute-start.3 = (bf16[2,128,1024]{2,1,0:T(8,128)(2,1)S(1)}, bf16[2,128,1024]{2,1,0:T(8,128)(2,1)S(1)}, u32[]{:S(2)}, u32[]{:S(2)}) collective-permute-start(bf16[2,128,1024]{2,1,0:T(8,128)(2,1)S(1)} %collective-permute-done.2), channel_id=1, source_target_pairs={{0,64},{64,128},{128,192},{192,256},{256,320},{320,384},{384,448},... | collective-permute-start | bytes 1572872 | tf_op jit(solution)/shard_map/ppermute | solution.py:34
  72.9 12.3 %copy-start = (bf16[2,128,1024]{2,1,0:T(8,128)(2,1)S(1)}, bf16[2,128,1024]{2,1,0:T(8,128)(2,1)}, u32[]{:S(2)}) copy-start(bf16[2,128,1024]{2,1,0:T(8,128)(2,1)} %param.11) | copy-start | bytes 1572868
  72.9 12.0 %collective-permute-start.6 = (bf16[2,128,1024]{2,1,0:T(8,128)(2,1)S(1)}, bf16[2,128,1024]{2,1,0:T(8,128)(2,1)S(1)}, u32[]{:S(2)}, u32[]{:S(2)}) collective-permute-start(bf16[2,128,1024]{2,1,0:T(8,128)(2,1)S(1)} %collective-permute-done.5), channel_id=1, source_target_pairs={{0,448},{64,0},{128,64},{192,128},{256,192},{320,256},{384,320},{4... | collective-permute-start | bytes 1572872 | tf_op jit(solution)/shard_map/ppermute | solution.py:36
  83.7 4.9 %copy-start.4 = (bf16[2,1024,128]{2,1,0:T(8,128)(2,1)S(1)}, bf16[2,1024,128]{2,1,0:T(8,128)(2,1)}, u32[]{:S(2)}) copy-start(bf16[2,1024,128]{2,1,0:T(8,128)(2,1)} %param.12) | copy-start | bytes 1572868
  85.4 3.2 %copy-start.3 = (bf16[2,2048,1024]{2,1,0:T(8,128)(2,1)}, bf16[2,2048,1024]{2,1,0:T(8,128)(2,1)S(1)}, u32[]{:S(2)}) copy-start(bf16[2,2048,1024]{2,1,0:T(8,128)(2,1)S(1)} %constant_dynamic-update-slice_fusion) | copy-start | bytes 25165828
  120.0 10.0 %copy-start.6 = (bf16[1024,128]{1,0:T(8,128)(2,1)S(1)}, bf16[1024,128]{1,0:T(8,128)(2,1)}, u32[]{:S(2)}) copy-start(bf16[1024,128]{1,0:T(8,128)(2,1)} %param.13) | copy-start | bytes 786436
  127.4 2.6 %copy-start.1 = (bf16[1024,2048]{1,0:T(8,128)(2,1)}, bf16[1024,2048]{1,0:T(8,128)(2,1)S(1)}, u32[]{:S(2)}) copy-start(bf16[1024,2048]{1,0:T(8,128)(2,1)S(1)} %convolution_convert_fusion) | copy-start | bytes 12582916
  127.4 3.3 %copy-start.5 = (bf16[2,1024,128]{2,1,0:T(8,128)(2,1)S(1)}, bf16[2,1024,128]{2,1,0:T(8,128)(2,1)}, u32[]{:S(2)}) copy-start(bf16[2,1024,128]{2,1,0:T(8,128)(2,1)} %param.12) | copy-start | bytes 1572868
  143.3 57.8 %copy-start.2 = (bf16[1024,2048]{1,0:T(8,128)(2,1)S(1)}, bf16[1024,2048]{1,0:T(8,128)(2,1)}, u32[]{:S(2)}) copy-start(bf16[1024,2048]{1,0:T(8,128)(2,1)} %copy-done.1) | copy-start | bytes 12582916
  143.4 57.8 %copy-start.7 = (bf16[1024,128]{1,0:T(8,128)(2,1)S(1)}, bf16[1024,128]{1,0:T(8,128)(2,1)}, u32[]{:S(2)}) copy-start(bf16[1024,128]{1,0:T(8,128)(2,1)} %param.10) | copy-start | bytes 786436
  143.4 52.2 %collective-permute-start.8 = (bf16[1024,128]{1,0:T(8,128)(2,1)S(1)}, bf16[1024,128]{1,0:T(8,128)(2,1)S(1)}, u32[]{:S(2)}, u32[]{:S(2)}) collective-permute-start(bf16[1024,128]{1,0:T(8,128)(2,1)S(1)} %constant_dynamic-slice_fusion), channel_id=1, source_target_pairs={{0,0},{1,1},{2,2},{3,3},{4,4},{5,5},{6,6},{7,7},{8,64},{9,65},{10,... | collective-permute-start | bytes 786440 | tf_op jit(solution)/shard_map/ppermute | solution.py:51
  150.1 51.0 %collective-permute-start.7 = (bf16[1024,128]{1,0:T(8,128)(2,1)S(1)}, bf16[1024,128]{1,0:T(8,128)(2,1)S(1)}, u32[]{:S(2)}, u32[]{:S(2)}) collective-permute-start(bf16[1024,128]{1,0:T(8,128)(2,1)S(1)} %constant_dynamic-slice_fusion.1), channel_id=1, source_target_pairs={{0,0},{1,1},{2,2},{3,3},{4,4},{5,5},{6,6},{7,7},{8,64},{9,65},{10,... | collective-permute-start | bytes 786440 | tf_op jit(solution)/shard_map/ppermute | solution.py:50
Sparse Core Ops, SparseCore 0:
  27.6 81.4 all-gather.1
